TPU v7x, 32 devices: a whole 2x2x4 slice. The times are simulated.
32 devices in a mesh: own: 8 (over z, x), grp: 4 (over y, core).
Axes of the slice: x: 2, y: 2, z: 4, core: 2. Of those that a mesh axis runs over, the one named last changes fastest.
Arguments:
- panel: float32 [8, 4, 768, 768], P('own', 'grp'), may hold values from -6 to 6
- diag_inverse: float32 [8, 768, 768], P('own', 'grp'), as said below
- ancestor: float32 [8, 4, 768, 768], P('own', 'grp'), may hold values from -6 to 6
- live_blocks: int32 [8], P('own'), may hold values from 1 to 4
- pair_first: int32 [8, 4, 7], P('own', 'grp'), may hold values from 0 to 3
- pair_second: int32 [8, 4, 7], P('own', 'grp'), may hold values from 0 to 3
- pair_offset: int32 [8, 4, 7], P('own', 'grp'), may hold values from 0 to 4
Outputs:
- solved: float32 [8, 4, 768, 768], P('own', 'grp')
- updated: float32 [8, 4, 768, 768], P('own', 'grp')
Inputs may be any that keep to these rules, and one draw needn't show every extreme that they name: diag_inverse[s] is upper triangular with a positive diagonal.
All inputs are finite; a program needn't handle non-finite values.
Results may differ from a plain program's by a relative error of at most 0.0001.
Values sent between devices are 32-bit elements; how exact they have to be, the bound alone decides.
No kernel may reach another device: no remote copies, remote signals or barrier semaphores. Data moves between devices by JAX's collectives and lax.ppermute only.
A program may use at most 128 MiB of HBM per device.

v0:
```python
import jax
import jax.numpy as jnp
from jax import lax
from jax.sharding import PartitionSpec as P

REACH = 5


def passed_along(array, axis, by):
    size = lax.axis_size(axis)
    return lax.ppermute(array, axis, [(i, (i + by) % size) for i in range(size)])


def shards(panel, diag_inverse, ancestor, live_blocks, pair_first, pair_second, pair_offset):
    group_index = lax.axis_index("grp")
    factor = lax.all_gather(diag_inverse, "grp", axis=1, tiled=True)
    alive = (group_index < live_blocks[0]).astype(jnp.float32)
    solved = alive * jnp.dot(panel[0, 0], factor[0], precision=lax.Precision.HIGHEST)
    column = lax.all_gather(solved[None], "grp", axis=0, tiled=True)
    first = column[pair_first[0, 0]]
    second = column[pair_second[0, 0]]
    terms = jnp.einsum("pij,pkj->pik", first, second, precision=lax.Precision.HIGHEST)
    distances = jnp.arange(REACH, dtype=jnp.int32)
    weights = (pair_offset[0, 0][None, :] == distances[:, None]).astype(jnp.float32)
    outgoing = jnp.einsum("dp,pik->dik", weights, terms, precision=lax.Precision.HIGHEST)
    received = outgoing[0]
    for distance in range(1, REACH):
        received = received + passed_along(outgoing[distance], "own", distance)
    updated = ancestor[0, 0] - received
    return (solved[None, None], updated[None, None])


def solution(mesh):
    placed = (
        P("own", "grp", None, None),
        P("own", "grp", None),
        P("own", "grp", None, None),
        P("own"),
        P("own", "grp", None),
        P("own", "grp", None),
        P("own", "grp", None),
    )
    return jax.shard_map(
        shards,
        mesh=mesh,
        in_specs=placed,
        out_specs=(P("own", "grp", None, None), P("own", "grp", None, None)),
        check_vma=False,
    )
```

profile of v0, /device:TPU:2, one launch (start us, length us, event | category | flops | bytes accessed | tf_op | source)
XLA Modules:
  0.0 560.0 jit_solution(9005479224907114235)
XLA Ops:
  7.2 0.0 copy-start
  7.2 0.0 all-gather.4.cloned.1.call-start
  7.2 0.7 all-gather.4.cloned.1.call-update
  7.9 0.0 all-gather.6.cloned.1.call-start
  8.6 26.2 %all-gather.4.cloned.1.call-done = f32[1,768,768]{2,1,0:T(8,128)} async-done(((f32[1,192,768]{2,1,0:T(8,128)}), f32[1,768,768]{2,1,0:T(8,128)}) %all-gather.4.cloned.1.call-update) | async-done | bytes 2359312 | tf_op jit(solution)/shard_map/all_gather | solution.py:16
  34.9 0.0 copy-done
  34.9 8.9 %fusion.11 = f32[768,768]{1,0:T(8,128)} fusion(f32[1,768,768]{2,1,0:T(8,128)} %all-gather.4.cloned.1.call-done, f32[1,1,768,768]{3,2,1,0:T(8,128)S(1)} %copy-done, f32[]{:T(128)S(6)} %convert_element_type.4), kind=kOutput, calls=%fused_computation.18 | convolution fusion | flops 5436407808 | bytes 7077892 | tf_op jit(solution)/shard_map/dot_general | solution.py:18
  43.8 0.0 copy-start.5
  43.8 0.0 copy-start.6
  43.8 0.0 all-gather.6.cloned.1.call-update
  43.8 0.6 copy-done.5
  44.4 0.0 copy-done.6
  44.5 63.7 %all-gather.6.cloned.1.call-done = f32[3072,768]{1,0:T(8,128)} async-done(((f32[768,768]{1,0:T(8,128)}), f32[3072,768]{1,0:T(8,128)}) %all-gather.6.cloned.1.call-update) | async-done | bytes 9437200 | tf_op jit(solution)/shard_map/all_gather | solution.py:19
  108.2 11.8 %gather_fusion = f32[7,768,768]{2,1,0:T(8,128)} fusion(f32[4,768,768]{2,1,0:T(8,128)} %bitcast.58, s32[1024]{0:T(1024)S(1)} %pad_clamp_fusion.1), kind=kCustom, calls=%fused_computation | custom fusion | bytes 33030172 | tf_op jit(solution)/shard_map/gather | solution.py:20
  120.0 11.6 %gather_fusion.1 = f32[7,768,768]{2,1,0:T(8,128)} fusion(f32[4,768,768]{2,1,0:T(8,128)} %bitcast.59, s32[1024]{0:T(1024)S(1)} %pad_clamp_fusion), kind=kCustom, calls=%fused_computation.1 | custom fusion | bytes 33030172 | tf_op jit(solution)/shard_map/gather | solution.py:21
  131.6 0.0 copy-start.4
  131.6 44.7 %fusion.22 = f32[7,768,768]{2,1,0:T(8,128)} fusion(f32[7,768,768]{2,1,0:T(8,128)} %gather_fusion, f32[7,768,768]{2,1,0:T(8,128)} %gather_fusion.1), kind=kOutput, calls=%fused_computation.29 | convolution fusion | flops 38050725888 | bytes 49545216 | tf_op jit(solution)/shard_map/pij,pkj->pik/dot_general | solution.py:22
  176.4 0.0 copy-done.4
  176.4 27.2 %fusion = f32[5,768,768]{2,0,1:T(8,128)} fusion(f32[7,768,768]{2,1,0:T(8,128)} %fusion.22, s32[7]{0:T(128)S(1)} %bitcast.65), kind=kOutput, calls=%fused_computation.2 | convolution fusion | flops 247726112 | bytes 28311580 | tf_op jit(solution)/shard_map/dp,pik->dik/dot_general | solution.py:25
  203.6 39.1 %fusion.21 = (f32[1,768,768]{2,0,1:T(1,128)}, f32[1,768,768]{2,0,1:T(1,128)S(1)}, f32[1,768,768]{2,0,1:T(1,128)S(1)}, f32[1,768,768]{2,0,1:T(1,128)S(1)}, f32[1,768,768]{2,0,1:T(1,128)S(1)}) fusion(f32[5,768,768]{2,0,1:T(8,128)} %fusion), kind=kLoop, calls=%fused_computation.28 | loop fusion | bytes 23592960 | tf_op jit(solution)/shard_map/slice | solution.py:26
  242.7 0.2 copy.39
  242.9 0.2 copy.40
  243.0 0.2 copy.41
  243.2 0.0 copy-start.2
  243.2 0.0 copy-start.3
  243.2 0.2 copy.38
  243.4 2.3 collective-permute-start.2
  245.7 0.5 collective-permute-start.3
  246.2 2.5 collective-permute-start
  248.7 0.4 collective-permute-start.1
  249.2 51.2 %collective-permute-done.2 = f32[768,768]{1,0:T(8,128)S(1)} collective-permute-done((f32[768,768]{1,0:T(8,128)S(1)}, f32[768,768]{1,0:T(8,128)S(1)}, u32[]{:S(2)}, u32[]{:S(2)}) %collective-permute-start.2) | collective-permute-done | bytes 2359328 | tf_op jit(solution)/shard_map/ppermute | solution.py:11
  300.4 250.5 %collective-permute-done.3 = f32[768,768]{1,0:T(8,128)S(1)} collective-permute-done((f32[768,768]{1,0:T(8,128)S(1)}, f32[768,768]{1,0:T(8,128)S(1)}, u32[]{:S(2)}, u32[]{:S(2)}) %collective-permute-start.3) | collective-permute-done | bytes 2359328 | tf_op jit(solution)/shard_map/ppermute | solution.py:11
  550.8 0.0 collective-permute-done
  550.8 0.0 collective-permute-done.1
  550.8 0.0 copy-done.2
  550.9 0.0 copy-done.3
  550.9 0.0 copy-start.1
  550.9 2.3 fusion.7
  553.2 0.0 copy-done.1
  (4 shorter events, 0.0 us)
Async XLA Ops:
  7.2 27.7 %copy-start = (f32[1,1,768,768]{3,2,1,0:T(8,128)S(1)}, f32[1,1,768,768]{3,2,1,0:T(8,128)}, u32[]{:S(2)}) copy-start(f32[1,1,768,768]{3,2,1,0:T(8,128)} %param.7) | copy-start | bytes 7077892
  7.2 27.7 %all-gather.4.cloned.1.call-start = ((), (), s32[]{:S(2)}) async-start(), calls=%async_computation | async-start | bytes 2949120 | tf_op jit(solution)/shard_map/all_gather | solution.py:16
  7.9 100.3 %all-gather.6.cloned.1.call-start = ((), (), s32[]{:S(2)}) async-start(), calls=%async_computation.1 | async-start | bytes 11796480 | tf_op jit(solution)/shard_map/all_gather | solution.py:19
  43.8 0.7 copy-start.5
  43.8 0.7 copy-start.6
  131.6 44.7 %copy-start.4 = (s32[1,1,7]{2,1,0:T(1,128)S(1)}, s32[1,1,7]{2,1,0:T(1,128)}, u32[]{:S(2)}) copy-start(s32[1,1,7]{2,1,0:T(1,128)} %param.13) | copy-start | bytes 88
  243.2 307.6 %copy-start.2 = (f32[1,768,768]{2,0,1:T(1,128)S(1)}, f32[1,768,768]{2,0,1:T(1,128)}, u32[]{:S(2)}) copy-start(f32[1,768,768]{2,0,1:T(1,128)} %get-tuple-element.2) | copy-start | bytes 7077892
  243.2 307.6 %copy-start.3 = (f32[1,1,768,768]{3,2,1,0:T(8,128)S(1)}, f32[1,1,768,768]{3,2,1,0:T(8,128)}, u32[]{:S(2)}) copy-start(f32[1,1,768,768]{3,2,1,0:T(8,128)} %param.9) | copy-start | bytes 7077892
  243.4 57.0 %collective-permute-start.2 = (f32[768,768]{1,0:T(8,128)S(1)}, f32[768,768]{1,0:T(8,128)S(1)}, u32[]{:S(2)}, u32[]{:S(2)}) collective-permute-start(f32[768,768]{1,0:T(8,128)S(1)} %bitcast.64), channel_id=1, source_target_pairs={{0,12},{4,16},{8,20},{12,24},{16,28},{20,0},{24,4},{28,8},{1,13},{... | collective-permute-start | bytes 7077896 | tf_op jit(solution)/shard_map/ppermute | solution.py:11
  245.7 305.2 %collective-permute-start.3 = (f32[768,768]{1,0:T(8,128)S(1)}, f32[768,768]{1,0:T(8,128)S(1)}, u32[]{:S(2)}, u32[]{:S(2)}) collective-permute-start(f32[768,768]{1,0:T(8,128)S(1)} %bitcast.63), channel_id=1, source_target_pairs={{0,16},{4,20},{8,24},{12,28},{16,0},{20,4},{24,8},{28,12},{1,17},{... | collective-permute-start | bytes 7077896 | tf_op jit(solution)/shard_map/ppermute | solution.py:11
  246.2 304.7 %collective-permute-start = (f32[768,768]{1,0:T(8,128)S(1)}, f32[768,768]{1,0:T(8,128)S(1)}, u32[]{:S(2)}, u32[]{:S(2)}) collective-permute-start(f32[768,768]{1,0:T(8,128)S(1)} %bitcast.62), channel_id=1, source_target_pairs={{0,4},{4,8},{8,12},{12,16},{16,20},{20,24},{24,28},{28,0},{1,5},{5... | collective-permute-start | bytes 7077896 | tf_op jit(solution)/shard_map/ppermute | solution.py:11
  248.7 302.1 %collective-permute-start.1 = (f32[768,768]{1,0:T(8,128)S(1)}, f32[768,768]{1,0:T(8,128)S(1)}, u32[]{:S(2)}, u32[]{:S(2)}) collective-permute-start(f32[768,768]{1,0:T(8,128)S(1)} %bitcast.61), channel_id=1, source_target_pairs={{0,8},{4,12},{8,16},{12,20},{16,24},{20,28},{24,0},{28,4},{1,9},{5... | collective-permute-start | bytes 7077896 | tf_op jit(solution)/shard_map/ppermute | solution.py:11
  550.9 2.3 copy-start.1
Sparse Core Ops, SparseCore 0:
  9.5 25.2 all-gather.3
  43.9 64.2 all-gather.5
where the time goes:
time: 560 us
  waiting for transfers between devices  392 us (70%)
  matrix products  80.9 us (14%)
  local copies, waits for them, and re-layouts  63.9 us (11%)
  between operations  14.8 us (3%)
  starting transfers between devices  5.85 us (1%)
    ppermute x4, waiting for transfers between devices, passed_along(): lax.ppermute(array, axis, [(i, (i + by) % size) for i in range(size)])  302 us
    all_gather x1, waiting for transfers between devices, shards(): column = lax.all_gather(solved[None], 'grp', axis=0, tiled=True)  63.7 us
    dot_general x1, matrix products, shards(): jnp.einsum('pij,pkj->pik', first, second, precision=lax.Precision.HIGHEST)  44.7 us
    slice x1, local copies, waits for them, and re-layouts, shards(): received = outgoing[0]  39.1 us
    dot_general x1, matrix products, shards(): jnp.einsum('dp,pik->dik', weights, terms, precision=lax.Precision.HIGHEST)  27.2 us
    all_gather x1, waiting for transfers between devices, shards(): factor = lax.all_gather(diag_inverse, 'grp', axis=1, tiled=True)  26.2 us
    gather x1, local copies, waits for them, and re-layouts, shards(): first = column[pair_first[0, 0]]  11.8 us
    gather x1, local copies, waits for them, and re-layouts, shards(): second = column[pair_second[0, 0]]  11.6 us
  transfers between devices with their start and end apart: 6, of which 4 were waited for; matrix products, arithmetic and copies ran while one was open for 0% of the time, Pallas kernels for 0%

commit v1 on v0

v1 whole, which is shorter than its diff:
```python
import jax
import jax.numpy as jnp
from jax import lax
from jax.experimental import pallas as pl
from jax.experimental.pallas import tpu as pltpu
from jax.sharding import PartitionSpec as P


REACH = 5
CHUNKS = 3
GRANT = 40 * 2**20
IN_VMEM = pl.BlockSpec(memory_space=pltpu.VMEM)
IN_SMEM = pl.BlockSpec(memory_space=pltpu.SMEM)


def swapped(array, axis, by):
    size = lax.axis_size(axis)
    return lax.ppermute(array, axis, [(i, i ^ by) for i in range(size)])


def passed_along(array, axis, by):
    size = lax.axis_size(axis)
    return lax.ppermute(array, axis, [(i, (i + by) % size) for i in range(size)])


def everyone(array, axis):
    size = lax.axis_size(axis)
    held = {0: array}
    bit = size // 2
    while bit:
        for r in sorted(held):
            held[r ^ bit] = swapped(held[r], axis, bit)
        bit //= 2
    return [held[r] for r in range(size)]


def halves(value):
    high = value.astype(jnp.bfloat16)
    low = (value - high.astype(jnp.float32)).astype(jnp.bfloat16)
    return high, low


def dot(a, b, dims):
    return lax.dot_general(a, b, (dims, ((), ())), preferred_element_type=jnp.float32)


def product(a, b, dims):
    return dot(a[0], b[0], dims) + (dot(a[0], b[1], dims) + dot(a[1], b[0], dims))


def params(limit=GRANT):
    return pltpu.CompilerParams(vmem_limit_bytes=limit)


def factor_kernel(n, meta, *refs):
    factors, (high_out, low_out) = refs[:n], refs[n:]
    depth = factors[0].shape[0]
    for r in range(n):
        rows = pl.ds(pl.multiple_of((meta[0] ^ r) * depth, depth), depth)
        high_out[rows, :], low_out[rows, :] = halves(factors[r][...])


def split_factor(meta, factors):
    n, order = len(factors), factors[0].shape[1]
    return pl.pallas_call(
        lambda *refs: factor_kernel(n, *refs),
        out_shape=[pltpu.VMEM((order, order), jnp.bfloat16)] * 2,
        in_specs=[IN_SMEM] + [IN_VMEM] * n,
        out_specs=[IN_VMEM] * 2,
        cost_estimate=pl.CostEstimate(flops=order * order, bytes_accessed=8 * order * order, transcendentals=0),
        compiler_params=params(),
        name="factor",
    )(meta, *factors)


def solve_kernel(n, meta, *refs):
    panels, (f_high, f_low), (solved, high_out, low_out) = refs[:n], refs[n : n + 2], refs[-3:]
    _, order = panels[0].shape
    for r in range(n):
        alive = (meta[0] ^ r) < meta[1]
        high, low = halves(panels[r][...])
        for j in range(CHUNKS):
            upto, cols = slice(0, (j + 1) * (order // CHUNKS)), pl.ds(j * (order // CHUNKS), order // CHUNKS)
            value = product((high[:, upto], low[:, upto]), (f_high[upto, cols], f_low[upto, cols]), ((1,), (0,)))
            value = jnp.where(alive, value, 0.0)
            if r == 0:
                solved[:, cols] = value
            high_out[r, :, cols], low_out[r, :, cols] = halves(value)


def solve(meta, panels, factor):
    n = len(panels)
    rows, order = panels[0].shape
    return pl.pallas_call(
        lambda *refs: solve_kernel(n, *refs),
        out_shape=[jax.ShapeDtypeStruct((rows, order), jnp.float32)] + [pltpu.VMEM((n, rows, order), jnp.bfloat16)] * 2,
        in_specs=[IN_SMEM] + [IN_VMEM] * (n + 2),
        out_specs=[IN_VMEM] * 3,
        cost_estimate=pl.CostEstimate(flops=4 * n * rows * order * order, bytes_accessed=8 * n * rows * order, transcendentals=0),
        compiler_params=params(),
        name="solve",
    )(meta, *panels, *factor)


def pair_kernel(left, right, pieces, pairs, *refs):
    highs, lows = refs[:pieces], refs[pieces : 2 * pieces]
    outs, total = refs[2 * pieces : 2 * pieces + REACH], refs[-1]
    count = pairs.shape[0] // 3
    total[...] = jnp.zeros_like(total)

    def stacked(refs, at, block):
        return jnp.concatenate([refs[k][block] for k in at]) if len(at) > 1 else refs[at[0]][block]

    def body(p, carry):
        a, b, d = pairs[p], pairs[count + p], pairs[2 * count + p]
        total[d] += product(
            (stacked(highs, left, a), stacked(lows, left, a)),
            (stacked(highs, right, b), stacked(lows, right, b)),
            ((1,), (1,)),
        )
        return carry

    lax.fori_loop(0, count, body, 0)
    for d in range(REACH):
        outs[d][...] = total[d]


def pair_sums(pairs, highs, lows, left, right):
    pieces, (_, rows, order) = len(highs), highs[0].shape
    shape = (len(left) * rows, len(right) * rows)
    return pl.pallas_call(
        lambda *refs: pair_kernel(left, right, pieces, *refs),
        out_shape=[pltpu.VMEM(shape, jnp.float32)] * REACH,
        in_specs=[IN_SMEM] + [IN_VMEM] * (2 * pieces),
        out_specs=[IN_VMEM] * REACH,
        scratch_shapes=[pltpu.VMEM((REACH,) + shape, jnp.float32)],
        cost_estimate=pl.CostEstimate(
            flops=2 * pairs.shape[0] * shape[0] * shape[1] * order, bytes_accessed=40 * shape[0] * shape[1], transcendentals=0
        ),
        compiler_params=params(),
        name="pairs",
    )(pairs, *highs, *lows)


def shards(panel, diag_inverse, ancestor, live_blocks, pair_first, pair_second, pair_offset):
    me = lax.axis_index("grp").astype(jnp.int32)
    even = lax.axis_index("own") % 2 == 0
    mine, before = panel[0, 0], ancestor[0, 0]
    order = mine.shape[0]
    step = order // CHUNKS
    meta = jnp.concatenate([me[None], live_blocks])
    pairs = jnp.concatenate([pair_first[0, 0] ^ me, pair_second[0, 0] ^ me, pair_offset[0, 0]])
    factor = split_factor(meta, everyone(diag_inverse[0], "grp"))
    solved, highs, lows, done = [], [], [], {}
    for c in range(CHUNKS):
        panels = everyone(mine[c * step : (c + 1) * step], "grp")
        value, high, low = solve(meta, panels, factor)
        solved.append(value)
        highs.append(high)
        lows.append(low)
        sets = [((c,), tuple(range(c)))] if c else []
        sets.append((tuple(range(c + 1)), (c,)))
        for part, (left, right) in enumerate(sets):
            name = f"{c}{part}"
            outs = pair_sums(pairs, highs, lows, left, right)
            third = swapped(outs[3], "own", 1)
            first = swapped(outs[1], "own", 1)
            far = passed_along(outs[4] + jnp.where(even, third, 0.0), "own", 2)
            near = passed_along(far + outs[2] + jnp.where(even, first, third), "own", 2)
            rows = slice(left[0] * step, (left[-1] + 1) * step)
            cols = slice(right[0] * step, (right[-1] + 1) * step)
            done[name] = before[rows, cols] - (near + outs[0] + jnp.where(even, 0.0, first))
    updated = done["00"]
    for c in range(1, CHUNKS):
        below, beside = done[f"{c}0"], done[f"{c}1"]
        updated = jnp.concatenate([jnp.concatenate([updated, below], 0), beside], 1)
    return (jnp.concatenate(solved)[None, None], updated[None, None])


def solution(mesh):
    placed = (
        P("own", "grp", None, None),
        P("own", "grp", None),
        P("own", "grp", None, None),
        P("own"),
        P("own", "grp", None),
        P("own", "grp", None),
        P("own", "grp", None),
    )
    return jax.shard_map(
        shards,
        mesh=mesh,
        in_specs=placed,
        out_specs=(P("own", "grp", None, None), P("own", "grp", None, None)),
        check_vma=False,
    )
```

time: 560 us -> 278 us (0.50)
  waiting for transfers between devices: 392 us -> 187 us
  matrix products: 80.9 us -> 0 us
  local copies, waits for them, and re-layouts: 63.9 us -> 10.2 us
  Pallas kernels: 0 us -> 46.1 us
  starting transfers between devices: 5.85 us -> 25.5 us
  between operations: 14.8 us -> 1.67 us
    ppermute x4 -> x10, waiting for transfers between devices: 302 us -> 65.1 us  [passed_along(): lax.ppermute(array, axis, [(i, (i + by) % size) for i in range(size)])]
    ppermute x0 -> x22, waiting for transfers between devices: none -> 122 us  [swapped(): return lax.ppermute(array, axis, [(i, i ^ by) for i in range(size)])]
    all_gather x2 -> x0, waiting for transfers between devices: 89.9 us -> none  [the longest x1 63.7 us: shards(): column = lax.all_gather(solved[None], 'grp', axis=0, tiled=True)]
    dot_general x3 -> x0, matrix products: 80.9 us -> none  [the longest x1 44.7 us: shards(): jnp.einsum('pij,pkj->pik', first, second, precision=lax.Precision.HIGHEST)]
    pallas_call x0 -> x9, Pallas kernels: none -> 46.1 us  [the longest x5 30.6 us: pair_sums(): pl.pallas_call(lambda *refs: pair_kernel(left, right, pieces, *refs), out...]
    slice x1, local copies, waits for them, and re-layouts: 39.1 us -> 1.76 us  [shards(): panels = everyone(mine[c * step:(c + 1) * step], 'grp')]
    gather x2 -> x0, local copies, waits for them, and re-layouts: 23.5 us -> none  [the longest x1 11.8 us: shards(): first = column[pair_first[0, 0]]]
    ppermute x0 -> x22, starting transfers between devices: none -> 16 us  [swapped(): return lax.ppermute(array, axis, [(i, i ^ by) for i in range(size)])]
  transfers between devices with their start and end apart: 6 -> 32, of which waited for: 4 -> 20; matrix products, arithmetic and copies ran while one was open for 0% -> 2% of each run, Pallas kernels for 0% -> 7%
where the time goes in v1:
time: 278 us; the launch traced here: 277 us
  waiting for transfers between devices  187 us (67%)
  Pallas kernels  46.1 us (17%)
  starting transfers between devices  25.5 us (9%)
  local copies, waits for them, and re-layouts  10.2 us (4%)
  other arithmetic  5.65 us (2%)
    ppermute x22, waiting for transfers between devices, swapped(): return lax.ppermute(array, axis, [(i, i ^ by) for i in range(size)])  122 us
    ppermute x10, waiting for transfers between devices, passed_along(): lax.ppermute(array, axis, [(i, (i + by) % size) for i in range(size)])  65.1 us
    pallas_call x5, Pallas kernels, pair_sums(): pl.pallas_call(lambda *refs: pair_kernel(left, right, pieces, *refs), out...  30.6 us
    ppermute x22, starting transfers between devices, swapped(): return lax.ppermute(array, axis, [(i, i ^ by) for i in range(size)])  16 us
    pallas_call x3, Pallas kernels, solve(): pl.pallas_call(lambda *refs: solve_kernel(n, *refs), out_shape=[jax.Shape...  14 us
    ppermute x10, starting transfers between devices, passed_along(): lax.ppermute(array, axis, [(i, (i + by) % size) for i in range(size)])  9.53 us
    unnamed x38, local copies, waits for them, and re-layouts  8.43 us
  transfers between devices with their start and end apart: 32, of which 20 were waited for; matrix products, arithmetic and copies ran while one was open for 2% of the time, Pallas kernels for 7%

profile of v1, /device:TPU:2, one launch (start us, length us, event | category | flops | bytes accessed | tf_op | source)
XLA Modules:
  0.0 276.5 jit_solution(15967569726356412482)
XLA Ops:
  0.7 1.6 collective-permute-start.4
  2.2 1.8 slice_bitcast_fusion.2
  5.1 1.5 collective-permute-start.7
  6.6 10.5 %collective-permute-done.4.refs_3_ = f32[192,768]{1,0:T(8,128)S(1)} collective-permute-done((f32[192,768]{1,0:T(8,128)}, f32[192,768]{1,0:T(8,128)S(1)}, u32[]{:S(2)}, u32[]{:S(2)}) %collective-permute-start.4) | collective-permute-done | bytes 589856 | tf_op jit(solution)/shard_map/ppermute | solution.py:18
  17.1 1.5 collective-permute-start.10
  19.5 14.6 %collective-permute-done.1.refs_3_ = f32[256,768]{1,0:T(8,128)} collective-permute-done((f32[256,768]{1,0:T(8,128)S(1)}, f32[256,768]{1,0:T(8,128)}, u32[]{:S(2)}, u32[]{:S(2)}) %collective-permute-start.1) | collective-permute-done | bytes 786464 | tf_op jit(solution)/shard_map/ppermute | solution.py:18
  35.5 15.5 %collective-permute-done.7.refs_3_ = f32[256,768]{1,0:T(8,128)} collective-permute-done((f32[256,768]{1,0:T(8,128)S(1)}, f32[256,768]{1,0:T(8,128)}, u32[]{:S(2)}, u32[]{:S(2)}) %collective-permute-start.7) | collective-permute-done | bytes 786464 | tf_op jit(solution)/shard_map/ppermute | solution.py:18
  51.6 15.0 %collective-permute-done.10.refs_3_ = f32[256,768]{1,0:T(8,128)} collective-permute-done((f32[256,768]{1,0:T(8,128)S(1)}, f32[256,768]{1,0:T(8,128)}, u32[]{:S(2)}, u32[]{:S(2)}) %collective-permute-start.10) | collective-permute-done | bytes 786464 | tf_op jit(solution)/shard_map/ppermute | solution.py:18
  69.1 1.6 factor.1
  70.7 4.1 %solve.3 = (f32[256,768]{1,0:T(8,128)S(1)}, bf16[4,256,768]{2,1,0:T(8,128)(2,1)S(1)}, bf16[4,256,768]{2,1,0:T(8,128)(2,1)S(1)}) custom-call(s32[2]{0:T(128)S(1)} %pad_add_fusion.refs_0_, f32[256,768]{1,0:T(8,128)S(1)} %get-tuple-element.76.refs_1_, f32[256,768]{1,0:T(8,128)S(1)} %copy-done.4, f32[256,768]{1,0:T(8,128)} %collective-permute-done.1.refs_3_, ...), custom_call_target="tpu_custom_call" | custom-call | flops 2415919104 | bytes 6291456 | tf_op jit(solution)/shard_map/solve/pallas_call | solution.py:94
  74.8 5.5 %solve.4 = (f32[256,768]{1,0:T(8,128)S(1)}, bf16[4,256,768]{2,1,0:T(8,128)(2,1)S(1)}, bf16[4,256,768]{2,1,0:T(8,128)(2,1)S(1)}) custom-call(s32[2]{0:T(128)S(1)} %pad_add_fusion.refs_0_, f32[256,768]{1,0:T(8,128)S(1)} %get-tuple-element.78.refs_1_, f32[256,768]{1,0:T(8,128)} %collective-permute-done.6.refs_2_, f32[256,768]{1,0:T(8,128)} %collective-permute-done.7.refs_3_, ...), custom_call_target="tpu_custom_call" | custom-call | flops 2415919104 | bytes 6291456 | tf_op jit(solution)/shard_map/solve/pallas_call | solution.py:94
  80.3 4.4 %pairs.6 = (f32[256,256]{1,0:T(8,128)S(1)}, f32[256,256]{1,0:T(8,128)S(1)}, f32[256,256]{1,0:T(8,128)S(1)}, f32[256,256]{1,0:T(8,128)S(1)}, f32[256,256]{1,0:T(8,128)S(1)}) custom-call(s32[21]{0:T(128)S(1)} %pad_add_fusion.1.refs_0_, bf16[4,256,768]{2,1,0:T(8,128)(2,1)S(1)} %get-tuple-element.43.refs_1_, bf16[4,256,768]{2,1,0:T(8,128)(2,1)S(1)} %get-tuple-element.50.refs_2_, ...), custom_call_target="tpu_custom_call" | custom-call | flops 2113929216 | bytes 2621440 | tf_op jit(solution)/shard_map/pairs/pallas_call | solution.py:131
  84.8 4.4 %solve.5 = (f32[256,768]{1,0:T(8,128)S(1)}, bf16[4,256,768]{2,1,0:T(8,128)(2,1)S(1)}, bf16[4,256,768]{2,1,0:T(8,128)(2,1)S(1)}) custom-call(s32[2]{0:T(128)S(1)} %pad_add_fusion.refs_0_, f32[256,768]{1,0:T(8,128)S(1)} %get-tuple-element.77.refs_1_, f32[256,768]{1,0:T(8,128)} %collective-permute-done.9.refs_2_, f32[256,768]{1,0:T(8,128)} %collective-permute-done.10.refs_3_, ...), custom_call_target="tpu_custom_call" | custom-call | flops 2415919104 | bytes 6291456 | tf_op jit(solution)/shard_map/solve/pallas_call | solution.py:94
  89.2 1.4 copy-done.14
  90.6 6.5 %pairs.8 = (f32[256,512]{1,0:T(8,128)S(1)}, f32[256,512]{1,0:T(8,128)S(1)}, f32[256,512]{1,0:T(8,128)S(1)}, f32[256,512]{1,0:T(8,128)S(1)}, f32[256,512]{1,0:T(8,128)S(1)}) custom-call(s32[21]{0:T(128)S(1)} %pad_add_fusion.1.refs_0_, bf16[4,256,768]{2,1,0:T(8,128)(2,1)S(1)} %get-tuple-element.43.refs_1_, bf16[4,256,768]{2,1,0:T(8,128)(2,1)S(1)} %get-tuple-element.50.refs_2_, ...), custom_call_target="tpu_custom_call" | custom-call | flops 4227858432 | bytes 5242880 | tf_op jit(solution)/shard_map/pairs/pallas_call | solution.py:131
  97.2 1.4 copy-done.6
  98.6 1.4 copy-done.9
  100.0 1.4 copy-done.12
  101.4 8.8 %pairs.9 = (f32[768,256]{1,0:T(8,128)S(1)}, f32[768,256]{1,0:T(8,128)S(1)}, f32[768,256]{1,0:T(8,128)S(1)}, f32[768,256]{1,0:T(8,128)S(1)}, f32[768,256]{1,0:T(8,128)S(1)}) custom-call(s32[21]{0:T(128)S(1)} %pad_add_fusion.1.refs_0_, bf16[4,256,768]{2,1,0:T(8,128)(2,1)S(1)} %copy-done.6, bf16[4,256,768]{2,1,0:T(8,128)(2,1)S(1)} %copy-done.12, ...), custom_call_target="tpu_custom_call" | custom-call | flops 6341787648 | bytes 7864320 | tf_op jit(solution)/shard_map/pairs/pallas_call | solution.py:131
  110.3 6.6 %pairs.7 = (f32[512,256]{1,0:T(8,128)S(1)}, f32[512,256]{1,0:T(8,128)S(1)}, f32[512,256]{1,0:T(8,128)S(1)}, f32[512,256]{1,0:T(8,128)S(1)}, f32[512,256]{1,0:T(8,128)S(1)}) custom-call(s32[21]{0:T(128)S(1)} %pad_add_fusion.1.refs_0_, bf16[4,256,768]{2,1,0:T(8,128)(2,1)S(1)} %copy-done.7, bf16[4,256,768]{2,1,0:T(8,128)(2,1)S(1)} %copy-done.12, ...), custom_call_target="tpu_custom_call" | custom-call | flops 4227858432 | bytes 5242880 | tf_op jit(solution)/shard_map/pairs/pallas_call | solution.py:131
  117.2 4.2 %pairs.5 = (f32[256,256]{1,0:T(8,128)S(1)}, f32[256,256]{1,0:T(8,128)S(1)}, f32[256,256]{1,0:T(8,128)S(1)}, f32[256,256]{1,0:T(8,128)S(1)}, f32[256,256]{1,0:T(8,128)S(1)}) custom-call(s32[21]{0:T(128)S(1)} %pad_add_fusion.1.refs_0_, bf16[4,256,768]{2,1,0:T(8,128)(2,1)S(1)} %copy-done.7, bf16[4,256,768]{2,1,0:T(8,128)(2,1)S(1)} %copy-done.10), custom_call_target="tpu_custom_call" | custom-call | flops 2113929216 | bytes 2621440 | tf_op jit(solution)/shard_map/pairs/pallas_call | solution.py:131
  121.5 1.8 collective-permute-start.18
  123.6 1.7 collective-permute-start.14
  125.6 1.6 maximum_bitcast_fusion
  127.1 1.7 collective-permute-start.20
  128.9 8.4 %collective-permute-done.12 = f32[256,256]{1,0:T(8,128)S(1)} collective-permute-done((f32[256,256]{1,0:T(8,128)S(1)}, f32[256,256]{1,0:T(8,128)S(1)}, u32[]{:S(2)}, u32[]{:S(2)}) %collective-permute-start.12) | collective-permute-done | bytes 262176 | tf_op jit(solution)/shard_map/ppermute | solution.py:18
  138.1 16.1 %collective-permute-done.24 = f32[256,512]{1,0:T(8,128)S(1)} collective-permute-done((f32[256,512]{1,0:T(8,128)S(1)}, f32[256,512]{1,0:T(8,128)S(1)}, u32[]{:S(2)}, u32[]{:S(2)}) %collective-permute-start.24) | collective-permute-done | bytes 524320 | tf_op jit(solution)/shard_map/ppermute | solution.py:18
  155.0 10.4 %collective-permute-done.20 = f32[512,256]{1,0:T(8,128)S(1)} collective-permute-done((f32[512,256]{1,0:T(8,128)S(1)}, f32[512,256]{1,0:T(8,128)S(1)}, u32[]{:S(2)}, u32[]{:S(2)}) %collective-permute-start.20) | collective-permute-done | bytes 524320 | tf_op jit(solution)/shard_map/ppermute | solution.py:18
  165.4 1.6 collective-permute-start.17
  167.8 5.8 %collective-permute-done.17 = f32[256,256]{1,0:T(8,128)S(1)} collective-permute-done((f32[256,256]{1,0:T(8,128)S(1)}, f32[256,256]{1,0:T(8,128)S(1)}, u32[]{:S(2)}, u32[]{:S(2)}) %collective-permute-start.17) | collective-permute-done | bytes 262176 | tf_op jit(solution)/shard_map/ppermute | solution.py:23
  173.7 8.5 %collective-permute-done.28 = f32[768,256]{1,0:T(8,128)S(1)} collective-permute-done((f32[768,256]{1,0:T(8,128)S(1)}, f32[768,256]{1,0:T(8,128)S(1)}, u32[]{:S(2)}, u32[]{:S(2)}) %collective-permute-start.28) | collective-permute-done | bytes 786464 | tf_op jit(solution)/shard_map/ppermute | solution.py:18
  182.2 1.6 collective-permute-start.25
  184.7 1.6 collective-permute-start.21
  186.3 7.2 %collective-permute-done.26 = f32[256,512]{1,0:T(8,128)S(1)} collective-permute-done((f32[256,512]{1,0:T(8,128)S(1)}, f32[256,512]{1,0:T(8,128)S(1)}, u32[]{:S(2)}, u32[]{:S(2)}) %collective-permute-start.26) | collective-permute-done | bytes 524320 | tf_op jit(solution)/shard_map/ppermute | solution.py:18
  193.5 1.6 collective-permute-start.29
  195.1 3.7 %collective-permute-done.25 = f32[256,512]{1,0:T(8,128)S(1)} collective-permute-done((f32[256,512]{1,0:T(8,128)S(1)}, f32[256,512]{1,0:T(8,128)S(1)}, u32[]{:S(2)}, u32[]{:S(2)}) %collective-permute-start.25) | collective-permute-done | bytes 524320 | tf_op jit(solution)/shard_map/ppermute | solution.py:23
  199.1 5.6 %collective-permute-done.22 = f32[512,256]{1,0:T(8,128)S(1)} collective-permute-done((f32[512,256]{1,0:T(8,128)S(1)}, f32[512,256]{1,0:T(8,128)S(1)}, u32[]{:S(2)}, u32[]{:S(2)}) %collective-permute-start.22) | collective-permute-done | bytes 524320 | tf_op jit(solution)/shard_map/ppermute | solution.py:18
  204.7 1.6 collective-permute-start.15
  206.3 3.8 %collective-permute-done.21 = f32[512,256]{1,0:T(8,128)S(1)} collective-permute-done((f32[512,256]{1,0:T(8,128)S(1)}, f32[512,256]{1,0:T(8,128)S(1)}, u32[]{:S(2)}, u32[]{:S(2)}) %collective-permute-start.21) | collective-permute-done | bytes 524320 | tf_op jit(solution)/shard_map/ppermute | solution.py:23
  210.2 10.4 %collective-permute-done.30 = f32[768,256]{1,0:T(8,128)S(1)} collective-permute-done((f32[768,256]{1,0:T(8,128)S(1)}, f32[768,256]{1,0:T(8,128)S(1)}, u32[]{:S(2)}, u32[]{:S(2)}) %collective-permute-start.30) | collective-permute-done | bytes 786464 | tf_op jit(solution)/shard_map/ppermute | solution.py:18
  220.6 1.6 collective-permute-start.23
  222.2 4.7 %collective-permute-done.29 = f32[768,256]{1,0:T(8,128)S(1)} collective-permute-done((f32[768,256]{1,0:T(8,128)S(1)}, f32[768,256]{1,0:T(8,128)S(1)}, u32[]{:S(2)}, u32[]{:S(2)}) %collective-permute-start.29) | collective-permute-done | bytes 786464 | tf_op jit(solution)/shard_map/ppermute | solution.py:23
  227.2 5.3 %collective-permute-done.19 = f32[256,256]{1,0:T(8,128)S(1)} collective-permute-done((f32[256,256]{1,0:T(8,128)S(1)}, f32[256,256]{1,0:T(8,128)S(1)}, u32[]{:S(2)}, u32[]{:S(2)}) %collective-permute-start.19) | collective-permute-done | bytes 262176 | tf_op jit(solution)/shard_map/ppermute | solution.py:23
  232.5 5.6 %collective-permute-done.15 = f32[256,256]{1,0:T(8,128)S(1)} collective-permute-done((f32[256,256]{1,0:T(8,128)S(1)}, f32[256,256]{1,0:T(8,128)S(1)}, u32[]{:S(2)}, u32[]{:S(2)}) %collective-permute-start.15) | collective-permute-done | bytes 262176 | tf_op jit(solution)/shard_map/ppermute | solution.py:23
  238.3 11.1 %collective-permute-done.27 = f32[256,512]{1,0:T(8,128)S(1)} collective-permute-done((f32[256,512]{1,0:T(8,128)S(1)}, f32[256,512]{1,0:T(8,128)S(1)}, u32[]{:S(2)}, u32[]{:S(2)}) %collective-permute-start.27) | collective-permute-done | bytes 524320 | tf_op jit(solution)/shard_map/ppermute | solution.py:23
  249.6 11.0 %collective-permute-done.23 = f32[512,256]{1,0:T(8,128)S(1)} collective-permute-done((f32[512,256]{1,0:T(8,128)S(1)}, f32[512,256]{1,0:T(8,128)S(1)}, u32[]{:S(2)}, u32[]{:S(2)}) %collective-permute-start.23) | collective-permute-done | bytes 524320 | tf_op jit(solution)/shard_map/ppermute | solution.py:23
  260.8 14.0 %collective-permute-done.31 = f32[768,256]{1,0:T(8,128)S(1)} collective-permute-done((f32[768,256]{1,0:T(8,128)S(1)}, f32[768,256]{1,0:T(8,128)S(1)}, u32[]{:S(2)}, u32[]{:S(2)}) %collective-permute-start.31) | collective-permute-done | bytes 786464 | tf_op jit(solution)/shard_map/ppermute | solution.py:23
  275.0 1.6 maximum_bitcast_fusion.1
  (83 shorter events, 11.6 us)
Async XLA Ops:
  0.6 4.0 %copy-start = (f32[1,192,768]{2,1,0:T(8,128)S(1)}, f32[1,192,768]{2,1,0:T(8,128)}, u32[]{:S(2)}) copy-start(f32[1,192,768]{2,1,0:T(8,128)} %param.8) | copy-start | bytes 1769476
  0.6 51.0 %copy-start.17 = (s32[1,1,7]{2,1,0:T(1,128)S(1)}, s32[1,1,7]{2,1,0:T(1,128)}, u32[]{:S(2)}) copy-start(s32[1,1,7]{2,1,0:T(1,128)} %param.12) | copy-start | bytes 88
  0.7 51.0 %copy-start.18 = (s32[1,1,7]{2,1,0:T(1,128)S(1)}, s32[1,1,7]{2,1,0:T(1,128)}, u32[]{:S(2)}) copy-start(s32[1,1,7]{2,1,0:T(1,128)} %param.11) | copy-start | bytes 88
  0.7 16.5 %collective-permute-start.4 = (f32[192,768]{1,0:T(8,128)}, f32[192,768]{1,0:T(8,128)S(1)}, u32[]{:S(2)}, u32[]{:S(2)}) collective-permute-start(f32[192,768]{1,0:T(8,128)} %bitcast.18), channel_id=1, source_target_pairs={{0,2},{1,3},{2,0},{3,1},{4,6},{5,7},{6,4},{7,5},{8,10},{9,11},{10,... | collective-permute-start | bytes 1769480 | tf_op jit(solution)/shard_map/ppermute | solution.py:18
  4.0 30.1 %collective-permute-start.1 = (f32[256,768]{1,0:T(8,128)S(1)}, f32[256,768]{1,0:T(8,128)}, u32[]{:S(2)}, u32[]{:S(2)}) collective-permute-start(f32[256,768]{1,0:T(8,128)S(1)} %get-tuple-element.76.refs_1_), channel_id=1, source_target_pairs={{0,2},{1,3},{2,0},{3,1},{4,6},{5,7},{6,4},{7,5},{8,10},{9,11},{10,... | collective-permute-start | bytes 2359304 | tf_op jit(solution)/shard_map/ppermute | solution.py:18
  4.6 14.1 %collective-permute-start.3 = (f32[192,768]{1,0:T(8,128)S(1)}, f32[192,768]{1,0:T(8,128)S(1)}, u32[]{:S(2)}, u32[]{:S(2)}) collective-permute-start(f32[192,768]{1,0:T(8,128)S(1)} %bitcast.19), channel_id=1, source_target_pairs={{0,1},{1,0},{2,3},{3,2},{4,5},{5,4},{6,7},{7,6},{8,9},{9,8},{10,11... | collective-permute-start | bytes 1769480 | tf_op jit(solution)/shard_map/ppermute | solution.py:18
  4.6 29.5 %collective-permute-start = (f32[256,768]{1,0:T(8,128)S(1)}, f32[256,768]{1,0:T(8,128)S(1)}, u32[]{:S(2)}, u32[]{:S(2)}) collective-permute-start(f32[256,768]{1,0:T(8,128)S(1)} %get-tuple-element.76.refs_1_), channel_id=1, source_target_pairs={{0,1},{1,0},{2,3},{3,2},{4,5},{5,4},{6,7},{7,6},{8,9},{9,8},{10,11... | collective-permute-start | bytes 2359304 | tf_op jit(solution)/shard_map/ppermute | solution.py:18
  5.1 45.9 %collective-permute-start.7 = (f32[256,768]{1,0:T(8,128)S(1)}, f32[256,768]{1,0:T(8,128)}, u32[]{:S(2)}, u32[]{:S(2)}) collective-permute-start(f32[256,768]{1,0:T(8,128)S(1)} %get-tuple-element.78.refs_1_), channel_id=1, source_target_pairs={{0,2},{1,3},{2,0},{3,1},{4,6},{5,7},{6,4},{7,5},{8,10},{9,11},{10,... | collective-permute-start | bytes 2359304 | tf_op jit(solution)/shard_map/ppermute | solution.py:18
  17.1 49.5 %collective-permute-start.10 = (f32[256,768]{1,0:T(8,128)S(1)}, f32[256,768]{1,0:T(8,128)}, u32[]{:S(2)}, u32[]{:S(2)}) collective-permute-start(f32[256,768]{1,0:T(8,128)S(1)} %get-tuple-element.77.refs_1_), channel_id=1, source_target_pairs={{0,2},{1,3},{2,0},{3,1},{4,6},{5,7},{6,4},{7,5},{8,10},{9,11},{10,... | collective-permute-start | bytes 2359304 | tf_op jit(solution)/shard_map/ppermute | solution.py:18
  19.5 47.2 %collective-permute-start.5 = (f32[192,768]{1,0:T(8,128)S(1)}, f32[192,768]{1,0:T(8,128)}, u32[]{:S(2)}, u32[]{:S(2)}) collective-permute-start(f32[192,768]{1,0:T(8,128)S(1)} %collective-permute-done.4.refs_3_), channel_id=1, source_target_pairs={{0,1},{1,0},{2,3},{3,2},{4,5},{5,4},{6,7},{7,6},{8,9},{9,8},{10,11... | collective-permute-start | bytes 1769480 | tf_op jit(solution)/shard_map/ppermute | solution.py:18
  34.1 36.6 %collective-permute-start.2 = (f32[256,768]{1,0:T(8,128)}, f32[256,768]{1,0:T(8,128)}, u32[]{:S(2)}, u32[]{:S(2)}) collective-permute-start(f32[256,768]{1,0:T(8,128)} %collective-permute-done.1.refs_3_), channel_id=1, source_target_pairs={{0,1},{1,0},{2,3},{3,2},{4,5},{5,4},{6,7},{7,6},{8,9},{9,8},{10,11... | collective-permute-start | bytes 2359304 | tf_op jit(solution)/shard_map/ppermute | solution.py:18
  35.0 39.8 %collective-permute-start.6 = (f32[256,768]{1,0:T(8,128)S(1)}, f32[256,768]{1,0:T(8,128)}, u32[]{:S(2)}, u32[]{:S(2)}) collective-permute-start(f32[256,768]{1,0:T(8,128)S(1)} %get-tuple-element.78.refs_1_), channel_id=1, source_target_pairs={{0,1},{1,0},{2,3},{3,2},{4,5},{5,4},{6,7},{7,6},{8,9},{9,8},{10,11... | collective-permute-start | bytes 2359304 | tf_op jit(solution)/shard_map/ppermute | solution.py:18
  50.9 23.9 %collective-permute-start.8 = (f32[256,768]{1,0:T(8,128)}, f32[256,768]{1,0:T(8,128)}, u32[]{:S(2)}, u32[]{:S(2)}) collective-permute-start(f32[256,768]{1,0:T(8,128)} %collective-permute-done.7.refs_3_), channel_id=1, source_target_pairs={{0,1},{1,0},{2,3},{3,2},{4,5},{5,4},{6,7},{7,6},{8,9},{9,8},{10,11... | collective-permute-start | bytes 2359304 | tf_op jit(solution)/shard_map/ppermute | solution.py:18
  66.7 18.1 %collective-permute-start.9 = (f32[256,768]{1,0:T(8,128)S(1)}, f32[256,768]{1,0:T(8,128)}, u32[]{:S(2)}, u32[]{:S(2)}) collective-permute-start(f32[256,768]{1,0:T(8,128)S(1)} %get-tuple-element.77.refs_1_), channel_id=1, source_target_pairs={{0,1},{1,0},{2,3},{3,2},{4,5},{5,4},{6,7},{7,6},{8,9},{9,8},{10,11... | collective-permute-start | bytes 2359304 | tf_op jit(solution)/shard_map/ppermute | solution.py:18
  66.7 18.1 %collective-permute-start.11 = (f32[256,768]{1,0:T(8,128)}, f32[256,768]{1,0:T(8,128)}, u32[]{:S(2)}, u32[]{:S(2)}) collective-permute-start(f32[256,768]{1,0:T(8,128)} %collective-permute-done.10.refs_3_), channel_id=1, source_target_pairs={{0,1},{1,0},{2,3},{3,2},{4,5},{5,4},{6,7},{7,6},{8,9},{9,8},{10,11... | collective-permute-start | bytes 2359304 | tf_op jit(solution)/shard_map/ppermute | solution.py:18
  69.1 1.6 copy-start.4
  74.8 14.4 %copy-start.5 = (bf16[4,256,768]{2,1,0:T(8,128)(2,1)}, bf16[4,256,768]{2,1,0:T(8,128)(2,1)S(1)}, u32[]{:S(2)}) copy-start(bf16[4,256,768]{2,1,0:T(8,128)(2,1)S(1)} %get-tuple-element.43.refs_1_) | copy-start | bytes 4718596
  74.8 14.4 %copy-start.8 = (bf16[4,256,768]{2,1,0:T(8,128)(2,1)}, bf16[4,256,768]{2,1,0:T(8,128)(2,1)S(1)}, u32[]{:S(2)}) copy-start(bf16[4,256,768]{2,1,0:T(8,128)(2,1)S(1)} %get-tuple-element.44.refs_2_.refs_3_.refs_4_) | copy-start | bytes 4718596
  80.3 4.5 %copy-start.13 = (bf16[4,256,768]{2,1,0:T(8,128)(2,1)}, bf16[4,256,768]{2,1,0:T(8,128)(2,1)S(1)}, u32[]{:S(2)}) copy-start(bf16[4,256,768]{2,1,0:T(8,128)(2,1)S(1)} %get-tuple-element.51.refs_4_.refs_5_) | copy-start | bytes 4718596
  80.3 8.9 %copy-start.11 = (bf16[4,256,768]{2,1,0:T(8,128)(2,1)}, bf16[4,256,768]{2,1,0:T(8,128)(2,1)S(1)}, u32[]{:S(2)}) copy-start(bf16[4,256,768]{2,1,0:T(8,128)(2,1)S(1)} %get-tuple-element.50.refs_2_) | copy-start | bytes 4718596
  89.2 1.4 copy-start.14
  90.6 6.5 %copy-start.15 = (bf16[4,256,768]{2,1,0:T(8,128)(2,1)S(1)}, bf16[4,256,768]{2,1,0:T(8,128)(2,1)}, u32[]{:S(2)}) copy-start(bf16[4,256,768]{2,1,0:T(8,128)(2,1)} %copy-done.13) | copy-start | bytes 4718596
  97.2 1.4 copy-start.6
  98.6 1.4 copy-start.9
  100.0 1.4 copy-start.12
  101.4 8.8 %copy-start.7 = (bf16[4,256,768]{2,1,0:T(8,128)(2,1)S(1)}, bf16[4,256,768]{2,1,0:T(8,128)(2,1)}, u32[]{:S(2)}) copy-start(bf16[4,256,768]{2,1,0:T(8,128)(2,1)} %copy-done.5) | copy-start | bytes 4718596
  101.4 8.9 %copy-start.10 = (bf16[4,256,768]{2,1,0:T(8,128)(2,1)S(1)}, bf16[4,256,768]{2,1,0:T(8,128)(2,1)}, u32[]{:S(2)}) copy-start(bf16[4,256,768]{2,1,0:T(8,128)(2,1)} %copy-done.8) | copy-start | bytes 4718596
  116.8 10.3 %collective-permute-start.16 = (f32[256,256]{1,0:T(8,128)S(1)}, f32[256,256]{1,0:T(8,128)S(1)}, u32[]{:S(2)}, u32[]{:S(2)}) collective-permute-start(f32[256,256]{1,0:T(8,128)S(1)} %get-tuple-element.53), channel_id=1, source_target_pairs={{0,4},{4,0},{8,12},{12,8},{16,20},{20,16},{24,28},{28,24},{1,5},{5... | collective-permute-start | bytes 786440 | tf_op jit(solution)/shard_map/ppermute | solution.py:18
  121.5 45.6 %collective-permute-start.18 = (f32[256,256]{1,0:T(8,128)S(1)}, f32[256,256]{1,0:T(8,128)S(1)}, u32[]{:S(2)}, u32[]{:S(2)}) collective-permute-start(f32[256,256]{1,0:T(8,128)S(1)} %get-tuple-element.55), channel_id=1, source_target_pairs={{0,4},{4,0},{8,12},{12,8},{16,20},{20,16},{24,28},{28,24},{1,5},{5... | collective-permute-start | bytes 786440 | tf_op jit(solution)/shard_map/ppermute | solution.py:18
  123.2 14.1 %collective-permute-start.12 = (f32[256,256]{1,0:T(8,128)S(1)}, f32[256,256]{1,0:T(8,128)S(1)}, u32[]{:S(2)}, u32[]{:S(2)}) collective-permute-start(f32[256,256]{1,0:T(8,128)S(1)} %get-tuple-element.46), channel_id=1, source_target_pairs={{0,4},{4,0},{8,12},{12,8},{16,20},{20,16},{24,28},{28,24},{1,5},{5... | collective-permute-start | bytes 786440 | tf_op jit(solution)/shard_map/ppermute | solution.py:18
  123.6 60.4 %collective-permute-start.14 = (f32[256,256]{1,0:T(8,128)S(1)}, f32[256,256]{1,0:T(8,128)S(1)}, u32[]{:S(2)}, u32[]{:S(2)}) collective-permute-start(f32[256,256]{1,0:T(8,128)S(1)} %get-tuple-element.48), channel_id=1, source_target_pairs={{0,4},{4,0},{8,12},{12,8},{16,20},{20,16},{24,28},{28,24},{1,5},{5... | collective-permute-start | bytes 786440 | tf_op jit(solution)/shard_map/ppermute | solution.py:18
  125.3 28.9 %collective-permute-start.24 = (f32[256,512]{1,0:T(8,128)S(1)}, f32[256,512]{1,0:T(8,128)S(1)}, u32[]{:S(2)}, u32[]{:S(2)}) collective-permute-start(f32[256,512]{1,0:T(8,128)S(1)} %get-tuple-element.65), channel_id=1, source_target_pairs={{0,4},{4,0},{8,12},{12,8},{16,20},{20,16},{24,28},{28,24},{1,5},{5... | collective-permute-start | bytes 1572872 | tf_op jit(solution)/shard_map/ppermute | solution.py:18
  127.1 38.3 %collective-permute-start.20 = (f32[512,256]{1,0:T(8,128)S(1)}, f32[512,256]{1,0:T(8,128)S(1)}, u32[]{:S(2)}, u32[]{:S(2)}) collective-permute-start(f32[512,256]{1,0:T(8,128)S(1)} %get-tuple-element.58), channel_id=1, source_target_pairs={{0,4},{4,0},{8,12},{12,8},{16,20},{20,16},{24,28},{28,24},{1,5},{5... | collective-permute-start | bytes 1572872 | tf_op jit(solution)/shard_map/ppermute | solution.py:18
  137.3 44.9 %collective-permute-start.28 = (f32[768,256]{1,0:T(8,128)S(1)}, f32[768,256]{1,0:T(8,128)S(1)}, u32[]{:S(2)}, u32[]{:S(2)}) collective-permute-start(f32[768,256]{1,0:T(8,128)S(1)} %get-tuple-element.70), channel_id=1, source_target_pairs={{0,4},{4,0},{8,12},{12,8},{16,20},{20,16},{24,28},{28,24},{1,5},{5... | collective-permute-start | bytes 2359304 | tf_op jit(solution)/shard_map/ppermute | solution.py:18
  154.2 39.3 %collective-permute-start.26 = (f32[256,512]{1,0:T(8,128)S(1)}, f32[256,512]{1,0:T(8,128)S(1)}, u32[]{:S(2)}, u32[]{:S(2)}) collective-permute-start(f32[256,512]{1,0:T(8,128)S(1)} %get-tuple-element.67), channel_id=1, source_target_pairs={{0,4},{4,0},{8,12},{12,8},{16,20},{20,16},{24,28},{28,24},{1,5},{5... | collective-permute-start | bytes 1572872 | tf_op jit(solution)/shard_map/ppermute | solution.py:18
  165.4 8.2 %collective-permute-start.17 = (f32[256,256]{1,0:T(8,128)S(1)}, f32[256,256]{1,0:T(8,128)S(1)}, u32[]{:S(2)}, u32[]{:S(2)}) collective-permute-start(f32[256,256]{1,0:T(8,128)S(1)} %select_add_fusion.7), channel_id=1, source_target_pairs={{0,8},{4,12},{8,16},{12,20},{16,24},{20,28},{24,0},{28,4},{1,9},{5... | collective-permute-start | bytes 786440 | tf_op jit(solution)/shard_map/ppermute | solution.py:23
  167.1 37.7 %collective-permute-start.22 = (f32[512,256]{1,0:T(8,128)S(1)}, f32[512,256]{1,0:T(8,128)S(1)}, u32[]{:S(2)}, u32[]{:S(2)}) collective-permute-start(f32[512,256]{1,0:T(8,128)S(1)} %get-tuple-element.60), channel_id=1, source_target_pairs={{0,4},{4,0},{8,12},{12,8},{16,20},{20,16},{24,28},{28,24},{1,5},{5... | collective-permute-start | bytes 1572872 | tf_op jit(solution)/shard_map/ppermute | solution.py:18
  173.6 11.1 %collective-permute-start.13 = (f32[256,256]{1,0:T(8,128)S(1)}, f32[256,256]{1,0:T(8,128)S(1)}, u32[]{:S(2)}, u32[]{:S(2)}) collective-permute-start(f32[256,256]{1,0:T(8,128)S(1)} %select_add_fusion.9), channel_id=1, source_target_pairs={{0,8},{4,12},{8,16},{12,20},{16,24},{20,28},{24,0},{28,4},{1,9},{5... | collective-permute-start | bytes 786440 | tf_op jit(solution)/shard_map/ppermute | solution.py:23
  182.2 16.6 %collective-permute-start.25 = (f32[256,512]{1,0:T(8,128)S(1)}, f32[256,512]{1,0:T(8,128)S(1)}, u32[]{:S(2)}, u32[]{:S(2)}) collective-permute-start(f32[256,512]{1,0:T(8,128)S(1)} %select_add_fusion.3), channel_id=1, source_target_pairs={{0,8},{4,12},{8,16},{12,20},{16,24},{20,28},{24,0},{28,4},{1,9},{5... | collective-permute-start | bytes 1572872 | tf_op jit(solution)/shard_map/ppermute | solution.py:23
  183.9 36.7 %collective-permute-start.30 = (f32[768,256]{1,0:T(8,128)S(1)}, f32[768,256]{1,0:T(8,128)S(1)}, u32[]{:S(2)}, u32[]{:S(2)}) collective-permute-start(f32[768,256]{1,0:T(8,128)S(1)} %get-tuple-element.72), channel_id=1, source_target_pairs={{0,4},{4,0},{8,12},{12,8},{16,20},{20,16},{24,28},{28,24},{1,5},{5... | collective-permute-start | bytes 2359304 | tf_op jit(solution)/shard_map/ppermute | solution.py:18
  184.7 25.3 %collective-permute-start.21 = (f32[512,256]{1,0:T(8,128)S(1)}, f32[512,256]{1,0:T(8,128)S(1)}, u32[]{:S(2)}, u32[]{:S(2)}) collective-permute-start(f32[512,256]{1,0:T(8,128)S(1)} %select_add_fusion.5), channel_id=1, source_target_pairs={{0,8},{4,12},{8,16},{12,20},{16,24},{20,28},{24,0},{28,4},{1,9},{5... | collective-permute-start | bytes 1572872 | tf_op jit(solution)/shard_map/ppermute | solution.py:23
  193.5 33.4 %collective-permute-start.29 = (f32[768,256]{1,0:T(8,128)S(1)}, f32[768,256]{1,0:T(8,128)S(1)}, u32[]{:S(2)}, u32[]{:S(2)}) collective-permute-start(f32[768,256]{1,0:T(8,128)S(1)} %select_add_fusion.1), channel_id=1, source_target_pairs={{0,8},{4,12},{8,16},{12,20},{16,24},{20,28},{24,0},{28,4},{1,9},{5... | collective-permute-start | bytes 2359304 | tf_op jit(solution)/shard_map/ppermute | solution.py:23
  198.8 33.7 %collective-permute-start.19 = (f32[256,256]{1,0:T(8,128)S(1)}, f32[256,256]{1,0:T(8,128)S(1)}, u32[]{:S(2)}, u32[]{:S(2)}) collective-permute-start(f32[256,256]{1,0:T(8,128)S(1)} %select_add_fusion.6), channel_id=1, source_target_pairs={{0,8},{4,12},{8,16},{12,20},{16,24},{20,28},{24,0},{28,4},{1,9},{5... | collective-permute-start | bytes 786440 | tf_op jit(solution)/shard_map/ppermute | solution.py:23
  204.7 33.4 %collective-permute-start.15 = (f32[256,256]{1,0:T(8,128)S(1)}, f32[256,256]{1,0:T(8,128)S(1)}, u32[]{:S(2)}, u32[]{:S(2)}) collective-permute-start(f32[256,256]{1,0:T(8,128)S(1)} %select_add_fusion.8), channel_id=1, source_target_pairs={{0,8},{4,12},{8,16},{12,20},{16,24},{20,28},{24,0},{28,4},{1,9},{5... | collective-permute-start | bytes 786440 | tf_op jit(solution)/shard_map/ppermute | solution.py:23
  210.1 39.3 %collective-permute-start.27 = (f32[256,512]{1,0:T(8,128)S(1)}, f32[256,512]{1,0:T(8,128)S(1)}, u32[]{:S(2)}, u32[]{:S(2)}) collective-permute-start(f32[256,512]{1,0:T(8,128)S(1)} %select_add_fusion.2), channel_id=1, source_target_pairs={{0,8},{4,12},{8,16},{12,20},{16,24},{20,28},{24,0},{28,4},{1,9},{5... | collective-permute-start | bytes 1572872 | tf_op jit(solution)/shard_map/ppermute | solution.py:23
  210.2 27.9 %copy-start.16 = (f32[1,1,768,768]{3,2,1,0:T(8,128)S(1)}, f32[1,1,768,768]{3,2,1,0:T(8,128)}, u32[]{:S(2)}) copy-start(f32[1,1,768,768]{3,2,1,0:T(8,128)} %param.9) | copy-start | bytes 7077892
  220.6 40.0 %collective-permute-start.23 = (f32[512,256]{1,0:T(8,128)S(1)}, f32[512,256]{1,0:T(8,128)S(1)}, u32[]{:S(2)}, u32[]{:S(2)}) collective-permute-start(f32[512,256]{1,0:T(8,128)S(1)} %select_add_fusion.4), channel_id=1, source_target_pairs={{0,8},{4,12},{8,16},{12,20},{16,24},{20,28},{24,0},{28,4},{1,9},{5... | collective-permute-start | bytes 1572872 | tf_op jit(solution)/shard_map/ppermute | solution.py:23
  227.1 47.6 %collective-permute-start.31 = (f32[768,256]{1,0:T(8,128)S(1)}, f32[768,256]{1,0:T(8,128)S(1)}, u32[]{:S(2)}, u32[]{:S(2)}) collective-permute-start(f32[768,256]{1,0:T(8,128)S(1)} %select_add_fusion), channel_id=1, source_target_pairs={{0,8},{4,12},{8,16},{12,20},{16,24},{20,28},{24,0},{28,4},{1,9},{5... | collective-permute-start | bytes 2359304 | tf_op jit(solution)/shard_map/ppermute | solution.py:23
  (3 other events, 2.8 us)
